TPU v7x, 128 devices: a whole 4x4x4 slice. The times are simulated.
128 devices in a mesh: basin: 32 (over z, x, core), tm: 4 (over y).
Axes of the slice: x: 4, y: 4, z: 4, core: 2. Of those that a mesh axis runs over, the one named last changes fastest.
Arguments:
- incidence: int32 [1024, 16, 128], P('basin'), may hold values 0 or 1
- row_gauge: int32 [16384], P('basin'), may hold values from 0 to 8191, as said below
- gauge_kernel: int32 [8192], P('basin'), may hold values from 0 to 31
- kernels: float32 [32, 128], replicated, may hold values from 0 to 0.0156
- observed: float32 [8192, 512], P('basin', 'tm'), may hold values from -8 to 8
- first_guess: float32 [131072, 512], P('basin', 'tm'), may hold values from -4 to 4
Outputs:
- inflows: float32 [131072, 512], P('basin', 'tm')
Inputs may be any that keep to these rules, and one draw needn't show every extreme that they name: `row_gauge`: the 512 slots of one index of basin name gauges of any one owner (gauges o * 256 to o * 256 + 255 belong to owner o) at most 32 times; in every draw one owner is named exactly 32 times by the slots of every index of basin.
All inputs are finite; a program needn't handle non-finite values. No bound on the sum of `incidence` on one device may be relied on, other than what follows from the above.
Results may differ from a plain program's by a relative error of at most 0.0001.
Values sent between devices are 32-bit elements; how exact they have to be, the bound alone decides.
A program may use at most 128 MiB of HBM per device.

v0:
```python
import functools

import jax
import jax.numpy as jnp
from jax import lax
from jax.experimental import pallas as pl
from jax.experimental.pallas import tpu as pltpu
from jax.sharding import PartitionSpec as P

ITERS = 3
CAP = 32
LANES = 128

HIGH = lax.Precision.HIGH
MESH = pl.DeviceIdType.MESH


def from_behind(x, axis, by):
    devices = lax.axis_size(axis)
    pairs = [(i, i + by) for i in range(devices) if 0 <= i + by < devices]
    return lax.ppermute(x, axis, pairs)


def lag_table(kernels, lag):
    classes, taps = kernels.shape
    rows, hours = lag.shape
    onehot = (lag.T[None, :, :] == jnp.arange(taps)[:, None, None]).astype(jnp.float32)
    picked = jnp.dot(kernels, onehot.reshape(taps, hours * rows), precision=HIGH)
    return picked.reshape(classes, hours, rows)


def class_mix(extended, table, selector):
    spread = lax.dot_general(extended, table, (((1,), (2,)), ((), ())), precision=lax.Precision.HIGH)
    return jnp.sum(spread * selector[:, :, None], axis=1)


def squared(values):
    return jnp.sum(values * values)


def squared_row(values):
    if values.shape[-1] == LANES:
        return jnp.sum(values * values, axis=0, keepdims=True)
    return as_row(squared(values))


def _total_body(x_ref, o_ref, tm_rows, all_rows, own_sem, tsend, trecv, bsend, brecv, *, nb, nt):
    me = lax.axis_index("basin")
    hb = lax.axis_index("tm")
    barrier = pltpu.get_barrier_semaphore()
    for j in range(1, nt):
        pl.semaphore_signal(barrier, inc=1, device_id=(me, lax.rem(hb + j, nt)), device_id_type=MESH)
    order = _peer_order(nb)
    if order is None:
        targets = [lax.rem(me + k, nb) for k in range(1, nb)]
        sources = [lax.rem(me + nb - k, nb) for k in range(1, nb)]
    else:
        targets = [_peer(me, o, 1) for o in order]
        sources = [_peer(me, o, -1) for o in order]
    for target in targets:
        pl.semaphore_signal(barrier, inc=1, device_id=(target, hb), device_id_type=MESH)
    pl.semaphore_wait(barrier, nt - 1 + nb - 1)

    own = pltpu.make_async_copy(x_ref, tm_rows.at[pl.ds(hb, 1)], own_sem.at[0])
    own.start()
    sends = []
    for j in range(1, nt):
        copy = pltpu.make_async_remote_copy(
            src_ref=x_ref, dst_ref=tm_rows.at[pl.ds(hb, 1)], send_sem=tsend.at[j], recv_sem=trecv.at[j],
            device_id=(me, lax.rem(hb + j, nt)), device_id_type=MESH,
        )
        copy.start()
        sends.append(copy)
    own.wait()
    for j in range(1, nt):
        sends[j - 1].wait_send()
        origin = lax.rem(hb + nt - j, nt)
        pltpu.make_async_remote_copy(
            src_ref=x_ref, dst_ref=tm_rows.at[pl.ds(origin, 1)], send_sem=tsend.at[j], recv_sem=trecv.at[j],
            device_id=(me, origin), device_id_type=MESH,
        ).wait_recv()

    own_block = pltpu.make_async_copy(tm_rows, all_rows.at[me], own_sem.at[1])
    own_block.start()
    blocks = []
    for i, target in enumerate(targets):
        copy = pltpu.make_async_remote_copy(
            src_ref=tm_rows, dst_ref=all_rows.at[me], send_sem=bsend.at[i], recv_sem=brecv.at[i],
            device_id=(target, hb), device_id_type=MESH,
        )
        copy.start()
        blocks.append(copy)
    own_block.wait()
    for i, source in enumerate(sources):
        blocks[i].wait_send()
        pltpu.make_async_remote_copy(
            src_ref=tm_rows, dst_ref=all_rows.at[source], send_sem=bsend.at[i], recv_sem=brecv.at[i],
            device_id=(source, hb), device_id_type=MESH,
        ).wait_recv()
    o_ref[...] = jnp.sum(all_rows[...].reshape(nb * nt, LANES), axis=0, keepdims=True)


def global_total(value):
    nb = lax.axis_size("basin")
    nt = lax.axis_size("tm")
    out = pl.pallas_call(
        functools.partial(_total_body, nb=nb, nt=nt),
        out_shape=jax.ShapeDtypeStruct((1, LANES), jnp.float32),
        in_specs=[pl.BlockSpec(memory_space=pltpu.VMEM)],
        out_specs=pl.BlockSpec(memory_space=pltpu.VMEM),
        scratch_shapes=[
            pltpu.VMEM((nt, LANES), jnp.float32),
            pltpu.VMEM((nb, nt, LANES), jnp.float32),
            pltpu.SemaphoreType.DMA((2,)),
            pltpu.SemaphoreType.DMA((nt,)),
            pltpu.SemaphoreType.DMA((nt,)),
            pltpu.SemaphoreType.DMA((nb,)),
            pltpu.SemaphoreType.DMA((nb,)),
        ],
        compiler_params=pltpu.CompilerParams(collective_id=0, has_side_effects=True),
    )(as_row(value))
    return jnp.sum(out)


def _peer_order(nb):
    if nb != 32:
        return None
    offsets = [(dz, dx, dc) for dz in range(4) for dx in range(4) for dc in range(2) if (dz, dx, dc) != (0, 0, 0)]
    return sorted(offsets, key=lambda o: (-(min(o[0], 4 - o[0]) + min(o[1], 4 - o[1])), o))


def _peer(me, offset, sign):
    if len(offset) == 1:
        return lax.rem(me + sign * offset[0] + 32 * 64, 32 * 64) % 32
    dz, dx, dc = offset
    z, x, c = me // 8, (me // 2) % 4, me % 2
    return ((z + sign * dz + 4) % 4) * 8 + ((x + sign * dx + 4) % 4) * 2 + (c + sign * dc + 2) % 2


def _exchange_body(x_ref, c_ref, landed, t_ref, carried, own_sem, send_sem, recv_sem, csend, crecv, *, nb):
    me = lax.axis_index("basin")
    hour_block = lax.axis_index("tm")
    order = _peer_order(nb)
    if order is None:
        order = [(k,) for k in range(1, nb)]
        targets = [lax.rem(me + k, nb) for k in range(1, nb)]
        sources = [lax.rem(me + nb - k, nb) for k in range(1, nb)]
    else:
        targets = [_peer(me, o, 1) for o in order]
        sources = [_peer(me, o, -1) for o in order]
    barrier = pltpu.get_barrier_semaphore()
    for target in targets:
        pl.semaphore_signal(barrier, inc=1, device_id=(target, hour_block), device_id_type=MESH)
    pl.semaphore_wait(barrier, nb - 1)
    own = pltpu.make_async_copy(x_ref.at[me], landed.at[me], own_sem.at[0])
    own.start()
    own_carry = pltpu.make_async_copy(c_ref, carried.at[pl.ds(me, 1)], own_sem.at[1])
    own_carry.start()
    copies = []
    for i, peer in enumerate(targets):
        copy = pltpu.make_async_remote_copy(
            src_ref=x_ref.at[peer],
            dst_ref=landed.at[me],
            send_sem=send_sem.at[i],
            recv_sem=recv_sem.at[i],
            device_id=(peer, hour_block),
            device_id_type=MESH,
        )
        copy.start()
        carry = pltpu.make_async_remote_copy(
            src_ref=c_ref,
            dst_ref=carried.at[pl.ds(me, 1)],
            send_sem=csend.at[i],
            recv_sem=crecv.at[i],
            device_id=(peer, hour_block),
            device_id_type=MESH,
        )
        carry.start()
        copies.append((copy, carry))
    own.wait()
    own_carry.wait()
    for i, source in enumerate(sources):
        copies[i][0].wait_send()
        copies[i][1].wait_send()
        pltpu.make_async_remote_copy(
            src_ref=x_ref.at[source],
            dst_ref=landed.at[source],
            send_sem=send_sem.at[i],
            recv_sem=recv_sem.at[i],
            device_id=(source, hour_block),
            device_id_type=MESH,
        ).wait_recv()
        pltpu.make_async_remote_copy(
            src_ref=c_ref,
            dst_ref=carried.at[pl.ds(source, 1)],
            send_sem=csend.at[i],
            recv_sem=crecv.at[i],
            device_id=(source, hour_block),
            device_id_type=MESH,
        ).wait_recv()
    t_ref[...] = jnp.sum(carried[...], axis=0, keepdims=True)


def as_row(value):
    if value.ndim == 2:
        return value
    return jnp.broadcast_to(value.astype(jnp.float32), (1, LANES))


def basin_exchange(x, carry, ident=1):
    nb = lax.axis_size("basin")
    total, hours = x.shape
    shaped = x.reshape(nb, total // nb, hours)
    out, summed = pl.pallas_call(
        functools.partial(_exchange_body, nb=nb),
        out_shape=(
            jax.ShapeDtypeStruct(shaped.shape, jnp.float32),
            jax.ShapeDtypeStruct((1, LANES), jnp.float32),
        ),
        in_specs=[pl.BlockSpec(memory_space=pltpu.VMEM)] * 2,
        out_specs=(pl.BlockSpec(memory_space=pltpu.VMEM),) * 2,
        scratch_shapes=[
            pltpu.VMEM((nb, LANES), jnp.float32),
            pltpu.SemaphoreType.DMA((2,)),
            pltpu.SemaphoreType.DMA((nb,)),
            pltpu.SemaphoreType.DMA((nb,)),
            pltpu.SemaphoreType.DMA((nb,)),
            pltpu.SemaphoreType.DMA((nb,)),
        ],
        compiler_params=pltpu.CompilerParams(collective_id=ident, has_side_effects=True),
    )(shaped, as_row(carry))
    return out.reshape(total, hours), summed


def _shift_body(x_ref, c_ref, o_ref, t_ref, carried, own_sem, dsend, drecv, csend, crecv, *, nt, by):
    basin = lax.axis_index("basin")
    me = lax.axis_index("tm")
    barrier = pltpu.get_barrier_semaphore()
    for k in range(1, nt):
        pl.semaphore_signal(
            barrier, inc=1, device_id=(basin, lax.rem(me + k, nt)), device_id_type=MESH
        )
    pl.semaphore_wait(barrier, nt - 1)

    target = me + by
    source = me - by
    has_target = jnp.logical_and(target >= 0, target < nt)
    has_source = jnp.logical_and(source >= 0, source < nt)
    data = pltpu.make_async_remote_copy(
        src_ref=x_ref,
        dst_ref=o_ref,
        send_sem=dsend,
        recv_sem=drecv,
        device_id=(basin, lax.rem(target + nt, nt)),
        device_id_type=MESH,
    )

    @pl.when(has_target)
    def _():
        data.start()

    own = pltpu.make_async_copy(c_ref, carried.at[pl.ds(me, 1)], own_sem)
    own.start()
    copies = []
    for k in range(1, nt):
        copy = pltpu.make_async_remote_copy(
            src_ref=c_ref,
            dst_ref=carried.at[pl.ds(me, 1)],
            send_sem=csend.at[k],
            recv_sem=crecv.at[k],
            device_id=(basin, lax.rem(me + k, nt)),
            device_id_type=MESH,
        )
        copy.start()
        copies.append(copy)
    own.wait()
    for k in range(1, nt):
        copies[k - 1].wait_send()
        origin = lax.rem(me + nt - k, nt)
        pltpu.make_async_remote_copy(
            src_ref=c_ref,
            dst_ref=carried.at[pl.ds(origin, 1)],
            send_sem=csend.at[k],
            recv_sem=crecv.at[k],
            device_id=(basin, origin),
            device_id_type=MESH,
        ).wait_recv()
    t_ref[...] = jnp.sum(carried[...], axis=0, keepdims=True)

    @pl.when(has_target)
    def _():
        data.wait_send()

    @pl.when(has_source)
    def _():
        data.wait_recv()

    @pl.when(jnp.logical_not(has_source))
    def _():
        o_ref[...] = jnp.zeros(o_ref.shape, o_ref.dtype)


def tm_shift(x, carry, by, ident):
    nt = lax.axis_size("tm")
    c = as_row(carry)
    out, summed = pl.pallas_call(
        functools.partial(_shift_body, nt=nt, by=by),
        out_shape=(
            jax.ShapeDtypeStruct(x.shape, jnp.float32),
            jax.ShapeDtypeStruct((1, LANES), jnp.float32),
        ),
        in_specs=[pl.BlockSpec(memory_space=pltpu.VMEM)] * 2,
        out_specs=(pl.BlockSpec(memory_space=pltpu.VMEM),) * 2,
        scratch_shapes=[
            pltpu.VMEM((nt, LANES), jnp.float32),
            pltpu.SemaphoreType.DMA(()),
            pltpu.SemaphoreType.DMA(()),
            pltpu.SemaphoreType.DMA(()),
            pltpu.SemaphoreType.DMA((nt,)),
            pltpu.SemaphoreType.DMA((nt,)),
        ],
        compiler_params=pltpu.CompilerParams(collective_id=ident, has_side_effects=True),
    )(x, c)
    return out, summed


def shards(incidence, row_gauge, gauge_kernel, kernels, observed, first_guess):
    weights = incidence.astype(jnp.float32)
    blocks, slots, width = weights.shape
    gauges_here, hours = observed.shape
    owners = lax.axis_size("basin")
    classes = kernels.shape[0]
    partials = blocks * slots
    outer = jnp.arange(2 * hours)[:, None]
    inner = jnp.arange(hours)[None, :]
    table_fwd = lag_table(kernels, inner + hours - outer)
    table_bwd = lag_table(kernels, outer - inner)
    selector = (gauge_kernel[:, None] == jnp.arange(classes)[None, :]).astype(jnp.float32)

    owner = row_gauge // gauges_here
    local = row_gauge % gauges_here
    hit = owner[:, None] == jnp.arange(owners)[None, :]
    rank = jnp.cumsum(hit.astype(jnp.int32), axis=0) - 1
    dest = owner * CAP + jnp.sum(jnp.where(hit, rank, 0), axis=1)
    entries = owners * CAP
    place = (jnp.arange(entries)[:, None] == dest[None, :]).astype(jnp.float32)
    sent_ids = jnp.full((entries,), -1, jnp.int32).at[dest].set(local)
    id_rows = jnp.zeros((owners, 8, hours), jnp.float32)
    id_rows = id_rows.at[:, 0, :CAP].set(sent_ids.reshape(owners, CAP).astype(jnp.float32))
    routing = {}

    def forward(field, carry=None):
        partial_value = jnp.einsum(
            "bjr,brt->bjt", weights, field.reshape(blocks, width, hours), precision=HIGH
        )
        outgoing = jnp.dot(place, partial_value.reshape(partials, hours), precision=HIGH)
        if "gather" not in routing:
            packed = jnp.concatenate([outgoing.reshape(owners, CAP, hours), id_rows], axis=1)
            landed, basin_sq = basin_exchange(packed.reshape(owners * (CAP + 8), hours), carry, 5)
            landed = landed.reshape(owners, CAP + 8, hours)
            got_ids = landed[:, CAP, :CAP].astype(jnp.int32).reshape(entries)
            routing["gather"] = (jnp.arange(gauges_here)[:, None] == got_ids[None, :]).astype(jnp.float32)
            incoming = landed[:, :CAP, :].reshape(entries, hours)
        else:
            incoming, basin_sq = basin_exchange(outgoing, squared_row(field))
        gather = routing["gather"]
        sums = jnp.dot(gather, incoming, precision=HIGH)
        earlier, total_sq = tm_shift(sums, basin_sq, 1, 2)
        return class_mix(jnp.concatenate([earlier, sums], axis=1), table_fwd, selector), jnp.sum(total_sq)

    def backward(series):
        later, tm_sq = tm_shift(series, squared_row(series), -1, 3)
        upstream = class_mix(jnp.concatenate([series, later], axis=1), table_bwd, selector)
        outgoing = jnp.dot(routing["gather"].T, upstream, precision=lax.Precision.HIGH)
        incoming, total_sq = basin_exchange(outgoing, tm_sq)
        rows = jnp.dot(place.T, incoming, precision=lax.Precision.HIGH)
        spread = jnp.einsum(
            "bjr,bjt->brt", weights, rows.reshape(blocks, slots, hours), precision=lax.Precision.HIGH
        )
        return spread.reshape(blocks * width, hours), jnp.sum(total_sq)

    start = observed - forward(first_guess, jnp.zeros((1, LANES), jnp.float32))[0]
    pulled_start, beta_sq = backward(start)
    beta = jnp.sqrt(beta_sq)
    u = start / beta
    pulled = pulled_start / beta
    forward_pulled, alpha_sq = forward(pulled)
    alpha = jnp.sqrt(alpha_sq)
    v = pulled / alpha
    w = v
    estimate = first_guess
    phibar = beta
    rhobar = alpha
    for step in range(ITERS):
        final = step == ITERS - 1
        p = forward_pulled / alpha - alpha * u
        if final:
            beta = jnp.sqrt(global_total(squared_row(p)))
        else:
            pulled_p, beta_sq = backward(p)
            beta = jnp.sqrt(beta_sq)
            pulled = pulled_p / beta - beta * v
            forward_pulled, alpha_next = forward(pulled)
            alpha_next = jnp.sqrt(alpha_next)
            v_next = pulled / alpha_next
        u = p / beta
        rho = jnp.sqrt(rhobar * rhobar + beta * beta)
        cosine = rhobar / rho
        sine = beta / rho
        phi = cosine * phibar
        phibar = sine * phibar
        estimate = estimate + phi / rho * w
        if not final:
            theta = sine * alpha_next
            rhobar = -cosine * alpha_next
            w = v_next - theta / rho * w
            v = v_next
            alpha = alpha_next
    return estimate


def solution(mesh):
    in_specs = (
        P("basin", None, None),
        P("basin"),
        P("basin"),
        P(),
        P("basin", "tm"),
        P("basin", "tm"),
    )
    out_specs = P("basin", "tm")
    return jax.shard_map(shards, mesh=mesh, in_specs=in_specs, out_specs=out_specs, check_vma=False)
```

profile of v0, /device:TPU:1, one launch (start us, length us, event | category | flops | bytes accessed | tf_op | source)
XLA Modules:
  0.0 297.1 jit_solution(13290789455695448652)
XLA Ops:
  0.0 0.7 add_select_fusion
  0.7 1.2 reduce-window.6
  2.3 2.6 fusion.58
  4.9 0.8 fusion.10
  5.7 2.4 scatter_custom_fusion
  8.2 0.9 select_maximum_fusion.x_ref
  9.6 20.1 %shard_map.64 = (f32[32,40,128]{2,1,0:T(8,128)}, f32[1,128]{1,0:T(1,128)}) custom-call(f32[32,40,128]{2,1,0:T(8,128)} %select_maximum_fusion.x_ref, f32[1,128]{1,0:T(1,128)} %broadcast_in_dim.27.c_ref), custom_call_target="tpu_custom_call" | custom-call | tf_op jit(solution)/shard_map/pallas_call | solution.py:214
  29.7 1.0 fusion.77
  30.7 1.1 slice.38
  31.8 1.1 fusion.26.x_ref
  32.9 8.4 %shard_map.65 = (f32[256,128]{1,0:T(8,128)}, f32[1,128]{1,0:T(1,128)}) custom-call(f32[256,128]{1,0:T(8,128)} %fusion.26.x_ref, f32[1,128]{1,0:T(1,128)} %get-tuple-element.45.c_ref), custom_call_target="tpu_custom_call" | custom-call | tf_op jit(solution)/shard_map/pallas_call | solution.py:306
  41.8 4.7 %fusion = f32[32768,32]{0,1:T(8,128)S(1)} fusion(f32[32,128]{1,0:T(8,128)S(1)} %copy-done, s32[32768]{0:T(1024)S(1)} %get-tuple-element.82), kind=kOutput, calls=%fused_computation.3 | convolution fusion | flops 809500672 | bytes 4341760 | tf_op jit(solution)/shard_map/dot_general | solution.py:28
  46.6 1.3 copy.39
  47.9 2.7 multiply_reduce_fusion.6
  50.6 1.2 multiply_reduce_fusion.13
  51.8 16.7 %shard_map.66 = (f32[256,128]{1,0:T(8,128)}, f32[1,128]{1,0:T(1,128)}) custom-call(f32[256,128]{1,0:T(8,128)} %get-tuple-element.76.x_ref, f32[1,128]{1,0:T(1,128)} %bitcast.174), custom_call_target="tpu_custom_call" | custom-call | tf_op jit(solution)/shard_map/pallas_call | solution.py:306
  68.5 4.7 %fusion.1 = f32[32768,32]{0,1:T(8,128)S(1)} fusion(f32[32,128]{1,0:T(8,128)S(1)} %copy-done, s32[32768]{0:T(1024)S(1)} %get-tuple-element.83), kind=kOutput, calls=%fused_computation.4 | convolution fusion | flops 809500672 | bytes 4341760 | tf_op jit(solution)/shard_map/dot_general | solution.py:28
  73.2 1.3 copy.41
  74.6 2.7 multiply_reduce_fusion.5
  77.3 1.0 slice_convert_fusion
  78.2 1.3 fusion.14.x_ref
  79.5 17.2 %shard_map.67 = (f32[32,32,128]{2,1,0:T(8,128)}, f32[1,128]{1,0:T(1,128)}) custom-call(f32[32,32,128]{2,1,0:T(8,128)} %fusion.14.x_ref, f32[1,128]{1,0:T(1,128)} %get-tuple-element.48.c_ref), custom_call_target="tpu_custom_call" | custom-call | tf_op jit(solution)/shard_map/pallas_call | solution.py:214
  97.1 1.8 fusion.79
  100.1 2.4 multiply_reduce_fusion.9
  102.6 0.9 fusion.27
  103.9 1.6 fusion.8.x_ref
  105.5 14.4 %shard_map.68 = (f32[32,32,128]{2,1,0:T(8,128)}, f32[1,128]{1,0:T(1,128)}) custom-call(f32[32,32,128]{2,1,0:T(8,128)} %fusion.8.x_ref, f32[1,128]{1,0:T(1,128)} %bitcast.176), custom_call_target="tpu_custom_call" | custom-call | tf_op jit(solution)/shard_map/pallas_call | solution.py:214
  119.9 2.1 fusion.25.x_ref
  122.1 8.2 %shard_map.69 = (f32[256,128]{1,0:T(8,128)}, f32[1,128]{1,0:T(1,128)}) custom-call(f32[256,128]{1,0:T(8,128)} %fusion.25.x_ref, f32[1,128]{1,0:T(1,128)} %get-tuple-element.52.c_ref), custom_call_target="tpu_custom_call" | custom-call | tf_op jit(solution)/shard_map/pallas_call | solution.py:306
  130.3 3.9 %multiply_reduce_fusion.4 = f32[256,128]{1,0:T(8,128)S(1)} fusion(f32[32,128,256]{2,1,0:T(8,128)} %bitcast.146, f32[256,32]{0,1:T(8,128)S(1)} %fusion.66, f32[256,128]{1,0:T(8,128)} %fusion.25.x_ref, f32[256,128]{1,0:T(8,128)} %get-tuple-element.54), kind=kOutput, calls=%fused_computation.11 | convolution fusion | flops 1612742656 | bytes 4620288 | tf_op jit(solution)/shard_map/dot_general | solution.py:33
  135.4 1.3 multiply_reduce_fusion.12
  136.7 5.6 %shard_map.70 = (f32[256,128]{1,0:T(8,128)}, f32[1,128]{1,0:T(1,128)}) custom-call(f32[256,128]{1,0:T(8,128)} %get-tuple-element.74.x_ref, f32[1,128]{1,0:T(1,128)} %bitcast.172), custom_call_target="tpu_custom_call" | custom-call | tf_op jit(solution)/shard_map/pallas_call | solution.py:306
  142.3 4.3 %multiply_reduce_fusion.3 = f32[256,128]{1,0:T(8,128)S(1)} fusion(f32[32,128,256]{2,1,0:T(8,128)} %bitcast.150, f32[256,32]{0,1:T(8,128)S(1)} %fusion.66, f32[256,128]{1,0:T(8,128)} %get-tuple-element.55, f32[256,128]{1,0:T(8,128)} %get-tuple-element.74.x_ref), kind=kOutput, calls=%fused_computation.10 | convolution fusion | flops 1612742656 | bytes 4620288 | tf_op jit(solution)/shard_map/dot_general | solution.py:33
  146.6 1.4 fusion.13.x_ref
  148.0 17.1 %shard_map.71 = (f32[32,32,128]{2,1,0:T(8,128)}, f32[1,128]{1,0:T(1,128)}) custom-call(f32[32,32,128]{2,1,0:T(8,128)} %fusion.13.x_ref, f32[1,128]{1,0:T(1,128)} %get-tuple-element.56.c_ref), custom_call_target="tpu_custom_call" | custom-call | tf_op jit(solution)/shard_map/pallas_call | solution.py:214
  165.0 1.3 reduce_sum.208
  167.2 1.8 fusion.80
  169.0 4.0 %multiply_reduce_fusion.8 = (f32[128]{0:T(128)}, f32[32,128,128]{1,2,0:T(8,128)S(1)}) fusion(f32[32,128,128]{1,2,0:T(8,128)} %copy-done.9, f32[]{:T(128)S(6)} %multiply.19, f32[]{:T(128)S(6)} %sqrt.32, f32[32,16,128]{2,1,0:T(8,128)S(1)} %fusion.80, s32[32,16,128]{2,1,0:T(8,128)S(1)} %copy-done.5), kind=kOutput, calls=%fused_computation.28 | convolution fusion | flops 53542784 | bytes 4719112 | tf_op jit(solution)/shard_map/bjr,bjt->brt/dot_general | solution.py:377
  173.0 0.9 fusion.52
  174.0 1.6 fusion.6.x_ref
  175.6 14.6 %shard_map.72 = (f32[32,32,128]{2,1,0:T(8,128)}, f32[1,128]{1,0:T(1,128)}) custom-call(f32[32,32,128]{2,1,0:T(8,128)} %fusion.6.x_ref, f32[1,128]{1,0:T(1,128)} %bitcast.177), custom_call_target="tpu_custom_call" | custom-call | tf_op jit(solution)/shard_map/pallas_call | solution.py:214
  190.2 2.1 fusion.24.x_ref
  192.3 8.1 %shard_map.73 = (f32[256,128]{1,0:T(8,128)}, f32[1,128]{1,0:T(1,128)}) custom-call(f32[256,128]{1,0:T(8,128)} %fusion.24.x_ref, f32[1,128]{1,0:T(1,128)} %get-tuple-element.60.c_ref), custom_call_target="tpu_custom_call" | custom-call | tf_op jit(solution)/shard_map/pallas_call | solution.py:306
  200.4 4.0 %multiply_reduce_fusion.2 = f32[256,128]{1,0:T(8,128)S(1)} fusion(f32[32,128,256]{2,1,0:T(8,128)} %bitcast.147, f32[256,32]{0,1:T(8,128)S(1)} %fusion.66, f32[256,128]{1,0:T(8,128)} %fusion.24.x_ref, f32[256,128]{1,0:T(8,128)} %get-tuple-element.62), kind=kOutput, calls=%fused_computation.9 | convolution fusion | flops 1612742656 | bytes 4620288 | tf_op jit(solution)/shard_map/dot_general | solution.py:33
  205.6 1.2 multiply_reduce_fusion.11
  206.8 5.6 %shard_map.74 = (f32[256,128]{1,0:T(8,128)}, f32[1,128]{1,0:T(1,128)}) custom-call(f32[256,128]{1,0:T(8,128)} %get-tuple-element.72.x_ref, f32[1,128]{1,0:T(1,128)} %bitcast.173), custom_call_target="tpu_custom_call" | custom-call | tf_op jit(solution)/shard_map/pallas_call | solution.py:306
  212.4 4.1 %multiply_reduce_fusion.1 = f32[256,128]{1,0:T(8,128)S(1)} fusion(f32[32,128,256]{2,1,0:T(8,128)} %bitcast.151, f32[256,32]{0,1:T(8,128)S(1)} %fusion.66, f32[256,128]{1,0:T(8,128)} %get-tuple-element.63, f32[256,128]{1,0:T(8,128)} %get-tuple-element.72.x_ref), kind=kOutput, calls=%fused_computation.8 | convolution fusion | flops 1612742656 | bytes 4620288 | tf_op jit(solution)/shard_map/dot_general | solution.py:33
  216.6 1.3 fusion.12.x_ref
  217.9 16.9 %shard_map.75 = (f32[32,32,128]{2,1,0:T(8,128)}, f32[1,128]{1,0:T(1,128)}) custom-call(f32[32,32,128]{2,1,0:T(8,128)} %fusion.12.x_ref, f32[1,128]{1,0:T(1,128)} %get-tuple-element.64.c_ref), custom_call_target="tpu_custom_call" | custom-call | tf_op jit(solution)/shard_map/pallas_call | solution.py:214
  234.8 1.2 reduce_sum.214
  236.7 1.8 fusion.81
  238.5 2.4 multiply_reduce_fusion.7
  240.9 1.3 copy-done.4
  242.2 0.9 fusion.49
  243.2 1.6 fusion.4.x_ref
  244.8 14.5 %shard_map.76 = (f32[32,32,128]{2,1,0:T(8,128)}, f32[1,128]{1,0:T(1,128)}) custom-call(f32[32,32,128]{2,1,0:T(8,128)} %fusion.4.x_ref, f32[1,128]{1,0:T(1,128)} %bitcast.175), custom_call_target="tpu_custom_call" | custom-call | tf_op jit(solution)/shard_map/pallas_call | solution.py:214
  259.2 2.1 fusion.23.x_ref
  261.4 8.1 %shard_map.77 = (f32[256,128]{1,0:T(8,128)}, f32[1,128]{1,0:T(1,128)}) custom-call(f32[256,128]{1,0:T(8,128)} %fusion.23.x_ref, f32[1,128]{1,0:T(1,128)} %get-tuple-element.68.c_ref), custom_call_target="tpu_custom_call" | custom-call | tf_op jit(solution)/shard_map/pallas_call | solution.py:306
  269.5 4.0 %multiply_reduce_fusion = f32[256,128]{1,0:T(8,128)S(1)} fusion(f32[32,128,256]{2,1,0:T(8,128)} %bitcast.148, f32[256,32]{0,1:T(8,128)S(1)} %fusion.66, f32[256,128]{1,0:T(8,128)} %fusion.23.x_ref, f32[256,128]{1,0:T(8,128)} %get-tuple-element.70), kind=kOutput, calls=%fused_computation.7 | convolution fusion | flops 1612742656 | bytes 4620288 | tf_op jit(solution)/shard_map/dot_general | solution.py:33
  273.4 0.6 reduce_sum.216
  275.2 14.5 %shard_map.78 = f32[1,128]{1,0:T(1,128)} custom-call(f32[1,128]{1,0:T(1,128)} %bitcast.178), custom_call_target="tpu_custom_call" | custom-call | tf_op jit(solution)/shard_map/pallas_call | solution.py:106
  289.7 1.3 reduce_sum.219
  291.9 3.3 %broadcast_multiply_fusion = (f32[32,128,128]{1,2,0:T(8,128)S(1)}, f32[32,128,128]{1,2,0:T(8,128)S(1)}, f32[32,128,128]{1,2,0:T(8,128)S(1)}) fusion(f32[]{:T(128)S(6)} %div.169, f32[32,128,128]{1,2,0:T(8,128)} %copy-done.9, f32[]{:T(128)S(6)} %multiply.19, f32[]{:T(128)S(6)} %div.173, f32[32,128,128]{1,2,0:T(8,128)S(1)} %get-tuple-element.89, f32[]{:T(128)S(6)} %sqrt.34, ...), kind=kLoop, calls=%fused_computation.33 | loop fusion | flops 5242880 | bytes 12582944 | tf_op jit(solution)/shard_map/mul | solution.py:412
  295.2 1.7 bitcast_add_fusion
  (61 shorter events, 4.6 us)
Async XLA Ops:
  0.0 41.8 %copy-start = (f32[32,128]{1,0:T(8,128)S(1)}, f32[32,128]{1,0:T(8,128)}, u32[]{:S(2)}) copy-start(f32[32,128]{1,0:T(8,128)} %param.11) | copy-start | bytes 49156
  5.7 35.7 %copy-start.14 = (s32[256]{0:T(256)S(1)}, s32[256]{0:T(256)}, u32[]{:S(2)}) copy-start(s32[256]{0:T(256)} %param.10) | copy-start | bytes 3076
  46.5 1.3 copy-start.10
  46.5 1.3 copy-start.11
  47.8 2.7 copy-start.1
  47.9 2.7 copy-start.13
  73.2 1.3 copy-start.8
  73.2 1.3 copy-start.12
  74.5 2.7 copy-start.2
  77.2 22.9 %copy-start.5 = (s32[32,16,128]{2,1,0:T(8,128)S(1)}, s32[32,16,128]{2,1,0:T(8,128)}, u32[]{:S(2)}) copy-start(s32[32,16,128]{2,1,0:T(8,128)} %param.8) | copy-start | bytes 786436
  96.7 2.1 copy-start.16
  102.6 1.3 copy-start.9
  130.3 3.9 %copy-start.17 = (f32[1,128]{1,0:T(1,128)S(1)}, f32[1,128]{1,0:T(1,128)}, u32[]{:S(2)}) copy-start(f32[1,128]{1,0:T(1,128)} %get-tuple-element.53) | copy-start | bytes 1540
  200.4 4.0 %copy-start.18 = (f32[1,128]{1,0:T(1,128)S(1)}, f32[1,128]{1,0:T(1,128)}, u32[]{:S(2)}) copy-start(f32[1,128]{1,0:T(1,128)} %get-tuple-element.61) | copy-start | bytes 1540
  200.4 5.2 %copy-start.7 = (f32[256,128]{1,0:T(8,128)S(1)}, f32[256,128]{1,0:T(8,128)}, u32[]{:S(2)}) copy-start(f32[256,128]{1,0:T(8,128)} %get-tuple-element.74.x_ref) | copy-start | bytes 393220
  240.9 1.3 copy-start.4
  269.4 4.0 %copy-start.15 = (f32[1,128]{1,0:T(1,128)S(1)}, f32[1,128]{1,0:T(1,128)}, u32[]{:S(2)}) copy-start(f32[1,128]{1,0:T(1,128)} %get-tuple-element.69) | copy-start | bytes 1540
  269.4 5.2 %copy-start.6 = (f32[256,128]{1,0:T(8,128)S(1)}, f32[256,128]{1,0:T(8,128)}, u32[]{:S(2)}) copy-start(f32[256,128]{1,0:T(8,128)} %get-tuple-element.72.x_ref) | copy-start | bytes 393220
  291.9 3.3 %copy-start.3 = (f32[4096,128]{1,0:T(8,128)S(1)}, f32[4096,128]{1,0:T(8,128)}, u32[]{:S(2)}) copy-start(f32[4096,128]{1,0:T(8,128)} %param.13) | copy-start | bytes 6291460
where the time goes:
time: 301 us; the launch traced here: 297 us
  Pallas kernels  190 us (63%)
  matrix products  71.6 us (24%)
  other arithmetic  20.6 us (7%)
  local copies, waits for them, and re-layouts  9.15 us (3%)
  between operations  5.87 us (2%)
    pallas_call x7, Pallas kernels, basin_exchange(): pl.pallas_call(functools.partial(_exchange_body, nb=nb), out_shape=(jax.S...  115 us
    pallas_call x7, Pallas kernels, tm_shift(): pl.pallas_call(functools.partial(_shift_body, nt=nt, by=by), out_shape=(j...  60.7 us
    dot_general x7, matrix products, class_mix(): lax.dot_general(extended, table, (((1,), (2,)), ((), ())), precision=lax....  25.6 us
    pallas_call x1, Pallas kernels, global_total(): pl.pallas_call(functools.partial(_total_body, nb=nb, nt=nt), out_shape=ja...  14.5 us
    dot_general x2, matrix products, lag_table(): jnp.dot(kernels, onehot.reshape(taps, hours * rows), precision=HIGH)  9.37 us
    dot_general x3, matrix products, backward(): jnp.einsum('bjr,bjt->brt', weights, rows.reshape(blocks, slots, hours), p...  8.85 us
    dot_general x4, matrix products, forward(): sums = jnp.dot(gather, incoming, precision=HIGH)  7.51 us

commit v1 on v0

--- a/solution.py
+++ b/solution.py
@@ -167,6 +167,8 @@
             device_id_type=MESH,
         )
         copy.start()
+        copies.append([copy])
+    for i, peer in enumerate(targets):
         carry = pltpu.make_async_remote_copy(
             src_ref=c_ref,
             dst_ref=carried.at[pl.ds(me, 1)],
@@ -176,7 +178,7 @@
             device_id_type=MESH,
         )
         carry.start()
-        copies.append((copy, carry))
+        copies[i].append(carry)
     own.wait()
     own_carry.wait()
     for i, source in enumerate(sources):

time: 301 us -> 308 us (1.023)
  Pallas kernels: 190 us -> 197 us
    pallas_call x7, Pallas kernels: 115 us -> 123 us  [basin_exchange(): pl.pallas_call(functools.partial(_exchange_body, nb=nb), out_shape=(jax.S...]
where the time goes in v1:
time: 308 us; the launch traced here: 304 us
  Pallas kernels  197 us (64%)
  matrix products  71.6 us (23%)
  other arithmetic  20.6 us (7%)
  local copies, waits for them, and re-layouts  9.15 us (3%)
  between operations  5.87 us (2%)
    pallas_call x7, Pallas kernels, basin_exchange(): pl.pallas_call(functools.partial(_exchange_body, nb=nb), out_shape=(jax.S...  123 us
    pallas_call x7, Pallas kernels, tm_shift(): pl.pallas_call(functools.partial(_shift_body, nt=nt, by=by), out_shape=(j...  59.7 us
    dot_general x7, matrix products, class_mix(): lax.dot_general(extended, table, (((1,), (2,)), ((), ())), precision=lax....  25.6 us
    pallas_call x1, Pallas kernels, global_total(): pl.pallas_call(functools.partial(_total_body, nb=nb, nt=nt), out_shape=ja...  14.6 us
    dot_general x2, matrix products, lag_table(): jnp.dot(kernels, onehot.reshape(taps, hours * rows), precision=HIGH)  9.37 us
    dot_general x3, matrix products, backward(): jnp.einsum('bjr,bjt->brt', weights, rows.reshape(blocks, slots, hours), p...  8.85 us
    dot_general x4, matrix products, forward(): sums = jnp.dot(gather, incoming, precision=HIGH)  7.5 us

profile of v1, /device:TPU:1, one launch (start us, length us, event | category | flops | bytes accessed | tf_op | source)
XLA Modules:
  0.0 304.3 jit_solution(582668652499502762)
XLA Ops:
  0.0 0.7 add_select_fusion
  0.7 1.2 reduce-window.6
  2.3 2.6 fusion.58
  4.9 0.8 fusion.10
  5.7 2.4 scatter_custom_fusion
  8.2 0.9 select_maximum_fusion.x_ref
  9.6 20.9 %shard_map.64 = (f32[32,40,128]{2,1,0:T(8,128)}, f32[1,128]{1,0:T(1,128)}) custom-call(f32[32,40,128]{2,1,0:T(8,128)} %select_maximum_fusion.x_ref, f32[1,128]{1,0:T(1,128)} %broadcast_in_dim.27.c_ref), custom_call_target="tpu_custom_call" | custom-call | tf_op jit(solution)/shard_map/pallas_call | solution.py:216
  30.6 1.0 fusion.77
  31.6 1.1 slice.38
  32.7 1.1 fusion.26.x_ref
  33.8 8.2 %shard_map.65 = (f32[256,128]{1,0:T(8,128)}, f32[1,128]{1,0:T(1,128)}) custom-call(f32[256,128]{1,0:T(8,128)} %fusion.26.x_ref, f32[1,128]{1,0:T(1,128)} %get-tuple-element.45.c_ref), custom_call_target="tpu_custom_call" | custom-call | tf_op jit(solution)/shard_map/pallas_call | solution.py:308
  42.5 4.7 %fusion = f32[32768,32]{0,1:T(8,128)S(1)} fusion(f32[32,128]{1,0:T(8,128)S(1)} %copy-done, s32[32768]{0:T(1024)S(1)} %get-tuple-element.82), kind=kOutput, calls=%fused_computation.3 | convolution fusion | flops 809500672 | bytes 4341760 | tf_op jit(solution)/shard_map/dot_general | solution.py:28
  47.2 1.3 copy.39
  48.5 2.7 multiply_reduce_fusion.6
  51.2 1.2 multiply_reduce_fusion.13
  52.4 16.7 %shard_map.66 = (f32[256,128]{1,0:T(8,128)}, f32[1,128]{1,0:T(1,128)}) custom-call(f32[256,128]{1,0:T(8,128)} %get-tuple-element.76.x_ref, f32[1,128]{1,0:T(1,128)} %bitcast.174), custom_call_target="tpu_custom_call" | custom-call | tf_op jit(solution)/shard_map/pallas_call | solution.py:308
  69.2 4.7 %fusion.1 = f32[32768,32]{0,1:T(8,128)S(1)} fusion(f32[32,128]{1,0:T(8,128)S(1)} %copy-done, s32[32768]{0:T(1024)S(1)} %get-tuple-element.83), kind=kOutput, calls=%fused_computation.4 | convolution fusion | flops 809500672 | bytes 4341760 | tf_op jit(solution)/shard_map/dot_general | solution.py:28
  73.9 1.3 copy.41
  75.2 2.7 multiply_reduce_fusion.5
  77.9 1.0 slice_convert_fusion
  78.9 1.3 fusion.14.x_ref
  80.1 18.0 %shard_map.67 = (f32[32,32,128]{2,1,0:T(8,128)}, f32[1,128]{1,0:T(1,128)}) custom-call(f32[32,32,128]{2,1,0:T(8,128)} %fusion.14.x_ref, f32[1,128]{1,0:T(1,128)} %get-tuple-element.48.c_ref), custom_call_target="tpu_custom_call" | custom-call | tf_op jit(solution)/shard_map/pallas_call | solution.py:216
  98.5 1.8 fusion.79
  101.6 2.4 multiply_reduce_fusion.9
  104.0 0.9 fusion.27
  105.3 1.6 fusion.8.x_ref
  107.0 15.9 %shard_map.68 = (f32[32,32,128]{2,1,0:T(8,128)}, f32[1,128]{1,0:T(1,128)}) custom-call(f32[32,32,128]{2,1,0:T(8,128)} %fusion.8.x_ref, f32[1,128]{1,0:T(1,128)} %bitcast.176), custom_call_target="tpu_custom_call" | custom-call | tf_op jit(solution)/shard_map/pallas_call | solution.py:216
  122.8 2.1 fusion.25.x_ref
  125.0 8.0 %shard_map.69 = (f32[256,128]{1,0:T(8,128)}, f32[1,128]{1,0:T(1,128)}) custom-call(f32[256,128]{1,0:T(8,128)} %fusion.25.x_ref, f32[1,128]{1,0:T(1,128)} %get-tuple-element.52.c_ref), custom_call_target="tpu_custom_call" | custom-call | tf_op jit(solution)/shard_map/pallas_call | solution.py:308
  132.9 3.9 %multiply_reduce_fusion.4 = f32[256,128]{1,0:T(8,128)S(1)} fusion(f32[32,128,256]{2,1,0:T(8,128)} %bitcast.146, f32[256,32]{0,1:T(8,128)S(1)} %fusion.66, f32[256,128]{1,0:T(8,128)} %fusion.25.x_ref, f32[256,128]{1,0:T(8,128)} %get-tuple-element.54), kind=kOutput, calls=%fused_computation.11 | convolution fusion | flops 1612742656 | bytes 4620288 | tf_op jit(solution)/shard_map/dot_general | solution.py:33
  138.1 1.3 multiply_reduce_fusion.12
  139.3 5.6 %shard_map.70 = (f32[256,128]{1,0:T(8,128)}, f32[1,128]{1,0:T(1,128)}) custom-call(f32[256,128]{1,0:T(8,128)} %get-tuple-element.74.x_ref, f32[1,128]{1,0:T(1,128)} %bitcast.172), custom_call_target="tpu_custom_call" | custom-call | tf_op jit(solution)/shard_map/pallas_call | solution.py:308
  144.9 4.3 %multiply_reduce_fusion.3 = f32[256,128]{1,0:T(8,128)S(1)} fusion(f32[32,128,256]{2,1,0:T(8,128)} %bitcast.150, f32[256,32]{0,1:T(8,128)S(1)} %fusion.66, f32[256,128]{1,0:T(8,128)} %get-tuple-element.55, f32[256,128]{1,0:T(8,128)} %get-tuple-element.74.x_ref), kind=kOutput, calls=%fused_computation.10 | convolution fusion | flops 1612742656 | bytes 4620288 | tf_op jit(solution)/shard_map/dot_general | solution.py:33
  149.2 1.4 fusion.13.x_ref
  150.6 18.2 %shard_map.71 = (f32[32,32,128]{2,1,0:T(8,128)}, f32[1,128]{1,0:T(1,128)}) custom-call(f32[32,32,128]{2,1,0:T(8,128)} %fusion.13.x_ref, f32[1,128]{1,0:T(1,128)} %get-tuple-element.56.c_ref), custom_call_target="tpu_custom_call" | custom-call | tf_op jit(solution)/shard_map/pallas_call | solution.py:216
  168.8 1.3 reduce_sum.208
  171.0 1.8 fusion.80
  172.8 4.0 %multiply_reduce_fusion.8 = (f32[128]{0:T(128)}, f32[32,128,128]{1,2,0:T(8,128)S(1)}) fusion(f32[32,128,128]{1,2,0:T(8,128)} %copy-done.9, f32[]{:T(128)S(6)} %multiply.19, f32[]{:T(128)S(6)} %sqrt.32, f32[32,16,128]{2,1,0:T(8,128)S(1)} %fusion.80, s32[32,16,128]{2,1,0:T(8,128)S(1)} %copy-done.5), kind=kOutput, calls=%fused_computation.28 | convolution fusion | flops 53542784 | bytes 4719112 | tf_op jit(solution)/shard_map/bjr,bjt->brt/dot_general | solution.py:379
  176.8 0.9 fusion.52
  177.7 1.6 fusion.6.x_ref
  179.4 15.9 %shard_map.72 = (f32[32,32,128]{2,1,0:T(8,128)}, f32[1,128]{1,0:T(1,128)}) custom-call(f32[32,32,128]{2,1,0:T(8,128)} %fusion.6.x_ref, f32[1,128]{1,0:T(1,128)} %bitcast.177), custom_call_target="tpu_custom_call" | custom-call | tf_op jit(solution)/shard_map/pallas_call | solution.py:216
  195.2 2.1 fusion.24.x_ref
  197.4 7.8 %shard_map.73 = (f32[256,128]{1,0:T(8,128)}, f32[1,128]{1,0:T(1,128)}) custom-call(f32[256,128]{1,0:T(8,128)} %fusion.24.x_ref, f32[1,128]{1,0:T(1,128)} %get-tuple-element.60.c_ref), custom_call_target="tpu_custom_call" | custom-call | tf_op jit(solution)/shard_map/pallas_call | solution.py:308
  205.2 4.0 %multiply_reduce_fusion.2 = f32[256,128]{1,0:T(8,128)S(1)} fusion(f32[32,128,256]{2,1,0:T(8,128)} %bitcast.147, f32[256,32]{0,1:T(8,128)S(1)} %fusion.66, f32[256,128]{1,0:T(8,128)} %fusion.24.x_ref, f32[256,128]{1,0:T(8,128)} %get-tuple-element.62), kind=kOutput, calls=%fused_computation.9 | convolution fusion | flops 1612742656 | bytes 4620288 | tf_op jit(solution)/shard_map/dot_general | solution.py:33
  210.4 1.2 multiply_reduce_fusion.11
  211.6 5.6 %shard_map.74 = (f32[256,128]{1,0:T(8,128)}, f32[1,128]{1,0:T(1,128)}) custom-call(f32[256,128]{1,0:T(8,128)} %get-tuple-element.72.x_ref, f32[1,128]{1,0:T(1,128)} %bitcast.173), custom_call_target="tpu_custom_call" | custom-call | tf_op jit(solution)/shard_map/pallas_call | solution.py:308
  217.2 4.1 %multiply_reduce_fusion.1 = f32[256,128]{1,0:T(8,128)S(1)} fusion(f32[32,128,256]{2,1,0:T(8,128)} %bitcast.151, f32[256,32]{0,1:T(8,128)S(1)} %fusion.66, f32[256,128]{1,0:T(8,128)} %get-tuple-element.63, f32[256,128]{1,0:T(8,128)} %get-tuple-element.72.x_ref), kind=kOutput, calls=%fused_computation.8 | convolution fusion | flops 1612742656 | bytes 4620288 | tf_op jit(solution)/shard_map/dot_general | solution.py:33
  221.3 1.3 fusion.12.x_ref
  222.7 18.1 %shard_map.75 = (f32[32,32,128]{2,1,0:T(8,128)}, f32[1,128]{1,0:T(1,128)}) custom-call(f32[32,32,128]{2,1,0:T(8,128)} %fusion.12.x_ref, f32[1,128]{1,0:T(1,128)} %get-tuple-element.64.c_ref), custom_call_target="tpu_custom_call" | custom-call | tf_op jit(solution)/shard_map/pallas_call | solution.py:216
  240.8 1.2 reduce_sum.214
  242.7 1.8 fusion.81
  244.5 2.4 multiply_reduce_fusion.7
  246.9 1.3 copy-done.4
  248.2 0.9 fusion.49
  249.2 1.6 fusion.4.x_ref
  250.8 15.8 %shard_map.76 = (f32[32,32,128]{2,1,0:T(8,128)}, f32[1,128]{1,0:T(1,128)}) custom-call(f32[32,32,128]{2,1,0:T(8,128)} %fusion.4.x_ref, f32[1,128]{1,0:T(1,128)} %bitcast.175), custom_call_target="tpu_custom_call" | custom-call | tf_op jit(solution)/shard_map/pallas_call | solution.py:216
  266.6 2.1 fusion.23.x_ref
  268.7 7.8 %shard_map.77 = (f32[256,128]{1,0:T(8,128)}, f32[1,128]{1,0:T(1,128)}) custom-call(f32[256,128]{1,0:T(8,128)} %fusion.23.x_ref, f32[1,128]{1,0:T(1,128)} %get-tuple-element.68.c_ref), custom_call_target="tpu_custom_call" | custom-call | tf_op jit(solution)/shard_map/pallas_call | solution.py:308
  276.6 4.0 %multiply_reduce_fusion = f32[256,128]{1,0:T(8,128)S(1)} fusion(f32[32,128,256]{2,1,0:T(8,128)} %bitcast.148, f32[256,32]{0,1:T(8,128)S(1)} %fusion.66, f32[256,128]{1,0:T(8,128)} %fusion.23.x_ref, f32[256,128]{1,0:T(8,128)} %get-tuple-element.70), kind=kOutput, calls=%fused_computation.7 | convolution fusion | flops 1612742656 | bytes 4620288 | tf_op jit(solution)/shard_map/dot_general | solution.py:33
  280.5 0.6 reduce_sum.216
  282.3 14.6 %shard_map.78 = f32[1,128]{1,0:T(1,128)} custom-call(f32[1,128]{1,0:T(1,128)} %bitcast.178), custom_call_target="tpu_custom_call" | custom-call | tf_op jit(solution)/shard_map/pallas_call | solution.py:106
  296.9 1.3 reduce_sum.219
  299.1 3.3 %broadcast_multiply_fusion = (f32[32,128,128]{1,2,0:T(8,128)S(1)}, f32[32,128,128]{1,2,0:T(8,128)S(1)}, f32[32,128,128]{1,2,0:T(8,128)S(1)}) fusion(f32[]{:T(128)S(6)} %div.169, f32[32,128,128]{1,2,0:T(8,128)} %copy-done.9, f32[]{:T(128)S(6)} %multiply.19, f32[]{:T(128)S(6)} %div.173, f32[32,128,128]{1,2,0:T(8,128)S(1)} %get-tuple-element.89, f32[]{:T(128)S(6)} %sqrt.34, ...), kind=kLoop, calls=%fused_computation.33 | loop fusion | flops 5242880 | bytes 12582944 | tf_op jit(solution)/shard_map/mul | solution.py:414
  302.5 1.7 bitcast_add_fusion
  (61 shorter events, 4.6 us)
Async XLA Ops:
  0.0 42.5 %copy-start = (f32[32,128]{1,0:T(8,128)S(1)}, f32[32,128]{1,0:T(8,128)}, u32[]{:S(2)}) copy-start(f32[32,128]{1,0:T(8,128)} %param.11) | copy-start | bytes 49156
  5.7 36.3 %copy-start.14 = (s32[256]{0:T(256)S(1)}, s32[256]{0:T(256)}, u32[]{:S(2)}) copy-start(s32[256]{0:T(256)} %param.10) | copy-start | bytes 3076
  47.2 1.3 copy-start.10
  47.2 1.3 copy-start.11
  48.5 2.7 copy-start.1
  48.5 2.7 copy-start.13
  73.9 1.3 copy-start.8
  73.9 1.3 copy-start.12
  75.2 2.7 copy-start.2
  77.9 23.7 %copy-start.5 = (s32[32,16,128]{2,1,0:T(8,128)S(1)}, s32[32,16,128]{2,1,0:T(8,128)}, u32[]{:S(2)}) copy-start(s32[32,16,128]{2,1,0:T(8,128)} %param.8) | copy-start | bytes 786436
  98.1 2.1 copy-start.16
  104.0 1.3 copy-start.9
  132.9 3.9 %copy-start.17 = (f32[1,128]{1,0:T(1,128)S(1)}, f32[1,128]{1,0:T(1,128)}, u32[]{:S(2)}) copy-start(f32[1,128]{1,0:T(1,128)} %get-tuple-element.53) | copy-start | bytes 1540
  205.2 4.0 %copy-start.18 = (f32[1,128]{1,0:T(1,128)S(1)}, f32[1,128]{1,0:T(1,128)}, u32[]{:S(2)}) copy-start(f32[1,128]{1,0:T(1,128)} %get-tuple-element.61) | copy-start | bytes 1540
  205.2 5.2 %copy-start.7 = (f32[256,128]{1,0:T(8,128)S(1)}, f32[256,128]{1,0:T(8,128)}, u32[]{:S(2)}) copy-start(f32[256,128]{1,0:T(8,128)} %get-tuple-element.74.x_ref) | copy-start | bytes 393220
  246.9 1.3 copy-start.4
  276.6 4.0 %copy-start.15 = (f32[1,128]{1,0:T(1,128)S(1)}, f32[1,128]{1,0:T(1,128)}, u32[]{:S(2)}) copy-start(f32[1,128]{1,0:T(1,128)} %get-tuple-element.69) | copy-start | bytes 1540
  276.6 5.2 %copy-start.6 = (f32[256,128]{1,0:T(8,128)S(1)}, f32[256,128]{1,0:T(8,128)}, u32[]{:S(2)}) copy-start(f32[256,128]{1,0:T(8,128)} %get-tuple-element.72.x_ref) | copy-start | bytes 393220
  299.1 3.3 %copy-start.3 = (f32[4096,128]{1,0:T(8,128)S(1)}, f32[4096,128]{1,0:T(8,128)}, u32[]{:S(2)}) copy-start(f32[4096,128]{1,0:T(8,128)} %param.13) | copy-start | bytes 6291460
